TPU v7x, 256 devices: a whole 4x4x8 slice. The times are simulated.
256 devices in a mesh: expert: 64 (over z, x, core), tensor: 4 (over y).
Axes of the slice: x: 4, y: 4, z: 8, core: 2. Of those that a mesh axis runs over, the one named last changes fastest.
Arguments:
- tokens: bfloat16 [16384, 2048], P('expert', 'tensor'), may hold values from -6 to 6
- out_grads: bfloat16 [16384, 2048], P('expert', 'tensor'), may hold values from -6 to 6
- species: int32 [16384, 1], P('expert'), may hold values from 0 to 63; in each aligned block of 64 rows (0 to 63, 64 to 127, ...) at most 2 rows name the same one
- expert_table: int32 [64], replicated, may hold values from 0 to 63, each once
- gate_weight: bfloat16 [64, 2048, 4096], P('expert', None, 'tensor'), may hold values from -0.125 to 0.125
- up_weight: bfloat16 [64, 2048, 4096], P('expert', None, 'tensor'), may hold values from -0.125 to 0.125
- down_weight: bfloat16 [64, 4096, 2048], P('expert', 'tensor'), may hold values from -0.09375 to 0.09375
Outputs:
- token_grads: bfloat16 [16384, 2048], P('expert', 'tensor')
Inputs may be any that keep to these rules, and one draw needn't show every extreme that they name: In each aligned block of 64 rows no species occurs more than 2 times, and in some blocks one species occurs exactly 2 times. `expert_table`: each species has a different expert.
All inputs are finite; a program needn't handle non-finite values.
Results may differ from a plain program's by a relative error of at most 0.0095.
Values may be sent and summed in bfloat16 or wider, within the bound.
A program may use at most 64 MiB of HBM per device.

v0:
```python
import jax
import jax.numpy as jnp
from jax import lax
from jax.sharding import PartitionSpec as P


def expert_partial(expert_rows, expert_grads, gate_matrix, up_matrix, down_matrix):
    contract = (((1,), (1,)), ((), ()))
    gate_pre = jnp.dot(expert_rows, gate_matrix, preferred_element_type=jnp.float32)
    up_pre = jnp.dot(expert_rows, up_matrix, preferred_element_type=jnp.float32)
    hidden_grad = lax.dot_general(
        expert_grads, down_matrix, contract, preferred_element_type=jnp.float32
    )
    sigmoid_gate = jax.nn.sigmoid(gate_pre)
    up_grad = (hidden_grad * gate_pre * sigmoid_gate).astype(jnp.bfloat16)
    gate_grad = (
        hidden_grad * up_pre * sigmoid_gate * (1.0 + gate_pre * (1.0 - sigmoid_gate))
    ).astype(jnp.bfloat16)
    partial_sum = lax.dot_general(
        gate_grad, gate_matrix, contract, preferred_element_type=jnp.float32
    )
    return partial_sum + lax.dot_general(
        up_grad, up_matrix, contract, preferred_element_type=jnp.float32
    )


def per_device(tokens, out_grads, species, expert_table, gate_weight, up_weight, down_weight):
    tensor_size = lax.axis_size("tensor")
    tensor_index = lax.axis_index("tensor")
    experts = expert_table.shape[0]
    group_tokens_count = tokens.shape[0]
    rows_dev = group_tokens_count // tensor_size
    head_width = tokens.shape[1]
    model_width = head_width * tensor_size
    capacity = 2 * rows_dev // experts
    expert_ids = jnp.arange(experts, dtype=jnp.int32)
    species_hits = species == expert_ids[None, :]
    expert_of = jnp.sum(jnp.where(species_hits, expert_table[None, :], 0), axis=1).reshape(
        tensor_size, rows_dev
    )
    onehot = (expert_of[:, :, None] == expert_ids[None, None, :]).astype(jnp.int32)
    earlier = jnp.cumsum(onehot, axis=1) - onehot
    slot_of = jnp.sum(earlier * onehot, axis=2)
    place_of = expert_of * capacity + slot_of
    slot_ids = jnp.arange(experts * capacity, dtype=jnp.int32)
    select = (slot_ids[None, :, None] == place_of[:, None, :]).astype(jnp.bfloat16)
    group_select = select.reshape(tensor_size, experts, capacity, rows_dev)
    own_select = lax.dynamic_index_in_dim(select, tensor_index, 0, keepdims=False)
    group_tokens, group_grads = (
        lax.all_gather(tokens, "tensor", axis=1, tiled=True),
        lax.all_gather(out_grads, "tensor", axis=1, tiled=True),
    )
    packed_rows = jnp.einsum(
        "tecr,trd->etcd",
        group_select,
        group_tokens.reshape(tensor_size, rows_dev, model_width),
        preferred_element_type=jnp.float32,
    ).astype(jnp.bfloat16)
    packed_grads = jnp.einsum(
        "tecr,trd->etcd",
        group_select,
        group_grads.reshape(tensor_size, rows_dev, model_width),
        preferred_element_type=jnp.float32,
    ).astype(jnp.bfloat16)
    packed_rows = packed_rows.reshape(experts, tensor_size * capacity, model_width)
    packed_grads = packed_grads.reshape(experts, tensor_size * capacity, model_width)
    expert_rows, expert_grads = (
        lax.all_to_all(packed_rows, "expert", split_axis=0, concat_axis=0, tiled=True),
        lax.all_to_all(packed_grads, "expert", split_axis=0, concat_axis=0, tiled=True),
    )
    slot_count = expert_rows.shape[0] * expert_rows.shape[1]
    partial_sum = expert_partial(
        expert_rows.reshape(slot_count, model_width),
        expert_grads.reshape(slot_count, model_width),
        gate_weight[0],
        up_weight[0],
        down_weight[0],
    )
    summed = lax.psum_scatter(
        partial_sum.reshape(experts, tensor_size * capacity, model_width).astype(jnp.bfloat16),
        "tensor",
        scatter_dimension=1,
        tiled=True,
    )
    returned = lax.all_to_all(summed, "expert", split_axis=0, concat_axis=0, tiled=True)
    own_grads = lax.dot_general(
        own_select,
        returned.reshape(experts * capacity, model_width),
        (((0,), (0,)), ((), ())),
        preferred_element_type=jnp.float32,
    ).astype(jnp.bfloat16)
    token_grads = lax.all_to_all(own_grads, "tensor", split_axis=1, concat_axis=0, tiled=True)
    return token_grads


def solution(mesh):
    placed = (
        P("expert", "tensor"),
        P("expert", "tensor"),
        P("expert", None),
        P(),
        P("expert", None, "tensor"),
        P("expert", None, "tensor"),
        P("expert", "tensor", None),
    )
    return jax.shard_map(
        per_device, mesh=mesh, in_specs=placed, out_specs=P("expert", "tensor"), check_vma=False
    )
```

profile of v0, /device:TPU:1, one launch (start us, length us, event | category | flops | bytes accessed | tf_op | source)
XLA Modules:
  0.0 264.5 jit_solution(15965972787222262756)
XLA Ops:
  6.5 0.7 all-gather.3.cloned.1.call-update
  7.3 0.8 select_reduce_fusion.1
  8.0 0.1 reshape.41
  8.1 0.1 fusion.33
  8.2 0.1 reduce_window_sum.11
  8.4 0.2 select_reduce_fusion
  8.6 28.9 %all-gather.3.cloned.1.call-done = bf16[256,2048]{1,0:T(8,128)(2,1)} async-done(((bf16[256,512]{1,0:T(8,128)(2,1)}), bf16[256,2048]{1,0:T(8,128)(2,1)}) %all-gather.3.cloned.1.call-update) | async-done | bytes 1048592 | tf_op jit(solution)/shard_map/all_gather | solution.py:51
  37.6 2.0 convolution_convert_fusion.1
  39.5 2.5 copy.26
  42.0 12.7 %all-to-all-start = ((bf16[64,8,2048]{2,1,0:T(8,128)(2,1)}), bf16[64,8,2048]{2,1,0:T(8,128)(2,1)S(1)}, u32[]{:S(2)}, u32[]{:S(2)}) async-start(bf16[64,8,2048]{2,1,0:T(8,128)(2,1)} %copy.26), calls=%async_computation | async-start | bytes 4194304 | tf_op jit(solution)/shard_map/all_to_all | solution.py:69
  54.7 0.0 all-gather.5.cloned.1.call-start
  54.8 0.7 all-gather.5.cloned.1.call-update
  55.5 26.7 %all-gather.5.cloned.1.call-done = bf16[256,2048]{1,0:T(8,128)(2,1)} async-done(((bf16[256,512]{1,0:T(8,128)(2,1)}), bf16[256,2048]{1,0:T(8,128)(2,1)}) %all-gather.5.cloned.1.call-update) | async-done | bytes 1048592 | tf_op jit(solution)/shard_map/all_gather | solution.py:50
  82.2 2.0 convolution_convert_fusion
  84.2 2.5 copy.27
  86.6 17.8 %all-to-all-done = bf16[64,8,2048]{2,1,0:T(8,128)(2,1)S(1)} async-done(((bf16[64,8,2048]{2,1,0:T(8,128)(2,1)}), bf16[64,8,2048]{2,1,0:T(8,128)(2,1)S(1)}, u32[]{:S(2)}, u32[]{:S(2)}) %all-to-all-start) | async-done | bytes 2097184 | tf_op jit(solution)/shard_map/all_to_all | solution.py:69
  104.4 7.2 %all-to-all-start.1 = ((bf16[64,8,2048]{2,1,0:T(8,128)(2,1)}), bf16[64,8,2048]{2,1,0:T(8,128)(2,1)}, u32[]{:S(2)}, u32[]{:S(2)}) async-start(bf16[64,8,2048]{2,1,0:T(8,128)(2,1)} %copy.27), calls=%async_computation.1 | async-start | bytes 4194304 | tf_op jit(solution)/shard_map/all_to_all | solution.py:68
  111.6 0.2 reduce-scatter.2.cloned.1.call-start
  111.8 6.0 %fusion.8 = f32[512,1024]{1,0:T(8,128)} fusion(bf16[1,1024,2048]{2,1,0:T(8,128)(2,1)} %param.13, bf16[64,8,2048]{2,1,0:T(8,128)(2,1)S(1)} %all-to-all-done), kind=kOutput, calls=%fused_computation.8 | convolution fusion | flops 2147483648 | bytes 8388608 | tf_op jit(solution)/shard_map/dot_general | solution.py:11
  117.8 43.4 %all-to-all-done.1 = bf16[64,8,2048]{2,1,0:T(8,128)(2,1)} async-done(((bf16[64,8,2048]{2,1,0:T(8,128)(2,1)}), bf16[64,8,2048]{2,1,0:T(8,128)(2,1)}, u32[]{:S(2)}, u32[]{:S(2)}) %all-to-all-start.1) | async-done | bytes 2097184 | tf_op jit(solution)/shard_map/all_to_all | solution.py:68
  161.2 6.5 %fusion.2 = f32[512,1024]{1,0:T(8,128)} fusion(bf16[1,2048,1024]{2,1,0:T(8,128)(2,1)} %param.11, bf16[64,8,2048]{2,1,0:T(8,128)(2,1)} %all-to-all-done.1), kind=kOutput, calls=%fused_computation.2 | convolution fusion | flops 2147483648 | bytes 8388608 | tf_op jit(solution)/shard_map/dot_general | solution.py:9
  167.7 11.5 %fusion = f32[512,2048]{1,0:T(8,128)} fusion(bf16[1,2048,1024]{2,1,0:T(8,128)(2,1)} %param.11, f32[512,1024]{1,0:T(8,128)} %fusion.2, f32[512,1024]{1,0:T(8,128)S(1)} %copy-done, bf16[1,2048,1024]{2,1,0:T(8,128)(2,1)} %param.12, bf16[64,8,2048]{2,1,0:T(8,128)(2,1)} %all-to-all-done.1), kind=kOutput, calls=%fused_computation | convolution fusion | flops 4300210176 | bytes 18874368 | tf_op jit(solution)/shard_map/dot_general | solution.py:19
  179.2 6.5 %fusion.12 = bf16[64,8,2048]{2,1,0:T(8,128)(2,1)S(1)} fusion(f32[512,2048]{1,0:T(8,128)} %fusion, bf16[1,2048,1024]{2,1,0:T(8,128)(2,1)} %param.12, f32[512,1024]{1,0:T(8,128)S(1)} %copy-done, f32[512,1024]{1,0:T(8,128)} %fusion.2), kind=kOutput, calls=%fused_computation.13 | convolution fusion | flops 2152726528 | bytes 14680064 | tf_op jit(solution)/shard_map/dot_general | solution.py:22
  185.7 2.5 copy.28
  188.2 29.1 %reduce-scatter.2.cloned.1.call-done = bf16[64,2,2048]{2,0,1:T(8,128)(2,1)} async-done(((bf16[64,8,2048]{2,0,1:T(8,128)(2,1)}), bf16[64,2,2048]{2,0,1:T(8,128)(2,1)}) %reduce-scatter.2.cloned.1.call-update) | async-done | bytes 524304 | tf_op jit(solution)/shard_map/reduce_scatter | solution.py:79
  217.3 2.4 copy.29
  219.7 10.7 %all-to-all-start.2 = ((bf16[64,2,2048]{2,1,0:T(2,128)(2,1)}), bf16[64,2,2048]{2,1,0:T(2,128)(2,1)S(1)}, u32[]{:S(2)}, u32[]{:S(2)}) async-start(bf16[64,2,2048]{2,1,0:T(2,128)(2,1)} %copy.29), calls=%async_computation.3 | async-start | bytes 1048576 | tf_op jit(solution)/shard_map/all_to_all | solution.py:85
  230.4 17.7 %all-to-all-done.2 = bf16[64,2,2048]{2,1,0:T(2,128)(2,1)S(1)} async-done(((bf16[64,2,2048]{2,1,0:T(2,128)(2,1)}), bf16[64,2,2048]{2,1,0:T(2,128)(2,1)S(1)}, u32[]{:S(2)}, u32[]{:S(2)}) %all-to-all-start.2) | async-done | bytes 524320 | tf_op jit(solution)/shard_map/all_to_all | solution.py:85
  248.1 0.2 reshape.48
  248.3 0.3 convolution_convert_fusion.2
  248.6 8.6 %all_to_all.34 = bf16[64,4,512]{2,0,1:T(8,128)(2,1)S(1)} all-to-all(bf16[64,4,512]{2,0,1:T(8,128)(2,1)S(1)} %bitcast.69), channel_id=1, replica_groups=mesh['expert'=64,'tensor'=4] {'tensor'}, dimensions={1} | all-to-all | bytes 524288 | tf_op jit(solution)/shard_map/all_to_all | solution.py:92
  257.2 0.7 copy.37
  (8 shorter events, 0.1 us)
Async XLA Ops:
  6.5 31.0 %all-gather.3.cloned.1.call-start = ((), (), s32[]{:S(2)}) async-start(), calls=%async_computation.5 | async-start | bytes 1310720 | tf_op jit(solution)/shard_map/all_gather | solution.py:51
  42.0 62.4 %all-to-all-start = ((bf16[64,8,2048]{2,1,0:T(8,128)(2,1)}), bf16[64,8,2048]{2,1,0:T(8,128)(2,1)S(1)}, u32[]{:S(2)}, u32[]{:S(2)}) async-start(bf16[64,8,2048]{2,1,0:T(8,128)(2,1)} %copy.26), calls=%async_computation | async-start | bytes 4194304 | tf_op jit(solution)/shard_map/all_to_all | solution.py:69
  54.7 27.4 %all-gather.5.cloned.1.call-start = ((), (), s32[]{:S(2)}) async-start(), calls=%async_computation.6 | async-start | bytes 1310720 | tf_op jit(solution)/shard_map/all_gather | solution.py:50
  104.4 56.8 %all-to-all-start.1 = ((bf16[64,8,2048]{2,1,0:T(8,128)(2,1)}), bf16[64,8,2048]{2,1,0:T(8,128)(2,1)}, u32[]{:S(2)}, u32[]{:S(2)}) async-start(bf16[64,8,2048]{2,1,0:T(8,128)(2,1)} %copy.27), calls=%async_computation.1 | async-start | bytes 4194304 | tf_op jit(solution)/shard_map/all_to_all | solution.py:68
  111.6 105.7 %reduce-scatter.2.cloned.1.call-start = ((), (), s32[]{:S(2)}) async-start(), calls=%async_computation.7 | async-start | bytes 2621440 | tf_op jit(solution)/shard_map/reduce_scatter | solution.py:79
  117.8 49.9 %copy-start = (f32[512,1024]{1,0:T(8,128)S(1)}, f32[512,1024]{1,0:T(8,128)}, u32[]{:S(2)}) copy-start(f32[512,1024]{1,0:T(8,128)} %fusion.8) | copy-start | bytes 6291460
  219.7 28.4 %all-to-all-start.2 = ((bf16[64,2,2048]{2,1,0:T(2,128)(2,1)}), bf16[64,2,2048]{2,1,0:T(2,128)(2,1)S(1)}, u32[]{:S(2)}, u32[]{:S(2)}) async-start(bf16[64,2,2048]{2,1,0:T(2,128)(2,1)} %copy.29), calls=%async_computation.3 | async-start | bytes 1048576 | tf_op jit(solution)/shard_map/all_to_all | solution.py:85
Sparse Core Ops, SparseCore 0:
  9.1 28.3 all-gather.2
  57.4 24.7 all-gather.4
  188.4 28.8 reduce-scatter.1
where the time goes:
time: 265 us; the launch traced here: 264 us
  waiting for transfers between devices  165 us (62%)
  matrix products  34.7 us (13%)
  starting transfers between devices  30.9 us (12%)
  between operations  13.2 us (5%)
  local copies, waits for them, and re-layouts  10.8 us (4%)
  blocking collectives  8.61 us (3%)
    all_to_all x1, waiting for transfers between devices, per_device(): lax.all_to_all(packed_rows, 'expert', split_axis=0, concat_axis=0, tiled=...  43.4 us
    reduce_scatter x1, waiting for transfers between devices, per_device(): lax.psum_scatter(partial_sum.reshape(experts, tensor_size * capacity, mod...  29.1 us
    all_gather x1, waiting for transfers between devices, per_device(): lax.all_gather(out_grads, 'tensor', axis=1, tiled=True)  28.9 us
    all_gather x1, waiting for transfers between devices, per_device(): lax.all_gather(tokens, 'tensor', axis=1, tiled=True)  26.7 us
    all_to_all x1, waiting for transfers between devices, per_device(): lax.all_to_all(packed_grads, 'expert', split_axis=0, concat_axis=0, tiled...  17.8 us
    all_to_all x1, waiting for transfers between devices, per_device(): lax.all_to_all(summed, 'expert', split_axis=0, concat_axis=0, tiled=True)  17.7 us
    all_to_all x1, starting transfers between devices, per_device(): lax.all_to_all(packed_grads, 'expert', split_axis=0, concat_axis=0, tiled...  12.7 us
    dot_general x1, matrix products, expert_partial(): lax.dot_general(gate_grad, gate_matrix, contract, preferred_element_type=...  11.5 us
  transfers between devices with their start and end apart: 6, of which 6 were waited for; matrix products, arithmetic and copies ran while one was open for 4% of the time, Pallas kernels for 0%

commit v1 on v0

--- a/solution.py
+++ b/solution.py
@@ -2,6 +2,11 @@
 import jax.numpy as jnp
 from jax import lax
 from jax.sharding import PartitionSpec as P
+
+
+def gather_over(value, axis, dim):
+    repeated = jnp.stack([value] * lax.axis_size(axis))
+    return jnp.concatenate(lax.all_to_all(repeated, axis, 0, 0), axis=dim)
 
 
 def expert_partial(expert_rows, expert_grads, gate_matrix, up_matrix, down_matrix):
@@ -48,7 +53,7 @@
     own_select = lax.dynamic_index_in_dim(select, tensor_index, 0, keepdims=False)
     group_tokens, group_grads = (
         lax.all_gather(tokens, "tensor", axis=1, tiled=True),
-        lax.all_gather(out_grads, "tensor", axis=1, tiled=True),
+        gather_over(out_grads, "tensor", 1),
     )
     packed_rows = jnp.einsum(
         "tecr,trd->etcd",

time: 265 us -> 256 us (0.966)
  waiting for transfers between devices: 165 us -> 147 us
  starting transfers between devices: 30.9 us -> 37.2 us
  local copies, waits for them, and re-layouts: 10.8 us -> 14.5 us
    all_gather x1 -> x0, waiting for transfers between devices: 28.9 us -> none  [per_device(): lax.all_gather(out_grads, 'tensor', axis=1, tiled=True)]
    all_to_all x0 -> x1, waiting for transfers between devices: none -> 12.8 us  [gather_over(): return jnp.concatenate(lax.all_to_all(repeated, axis, 0, 0), axis=dim)]
    all_to_all x0 -> x1, starting transfers between devices: none -> 5 us  [gather_over(): return jnp.concatenate(lax.all_to_all(repeated, axis, 0, 0), axis=dim)]
    another operation x0 -> x2, local copies, waits for them, and re-layouts: none -> 2.84 us  [the longest x1 2.03 us: gather_over(): repeated = jnp.stack([value] * lax.axis_size(axis))]
where the time goes in v1:
time: 256 us; the launch traced here: 255 us
  waiting for transfers between devices  147 us (57%)
  starting transfers between devices  37.2 us (15%)
  matrix products  33.5 us (13%)
  local copies, waits for them, and re-layouts  14.5 us (6%)
  between operations  13.5 us (5%)
  blocking collectives  8.59 us (3%)
    all_to_all x1, waiting for transfers between devices, per_device(): lax.all_to_all(packed_rows, 'expert', split_axis=0, concat_axis=0, tiled=...  43.4 us
    reduce_scatter x1, waiting for transfers between devices, per_device(): lax.psum_scatter(partial_sum.reshape(experts, tensor_size * capacity, mod...  28.1 us
    all_gather x1, waiting for transfers between devices, per_device(): lax.all_gather(tokens, 'tensor', axis=1, tiled=True)  25.8 us
    all_to_all x1, waiting for transfers between devices, per_device(): lax.all_to_all(packed_grads, 'expert', split_axis=0, concat_axis=0, tiled...  18.7 us
    all_to_all x1, waiting for transfers between devices, per_device(): lax.all_to_all(summed, 'expert', split_axis=0, concat_axis=0, tiled=True)  17.7 us
    all_to_all x1, starting transfers between devices, per_device(): lax.all_to_all(packed_grads, 'expert', split_axis=0, concat_axis=0, tiled...  14 us
    all_to_all x1, waiting for transfers between devices, gather_over(): return jnp.concatenate(lax.all_to_all(repeated, axis, 0, 0), axis=dim)  12.8 us
    dot_general x1, matrix products, expert_partial(): lax.dot_general(gate_grad, gate_matrix, contract, preferred_element_type=...  11.5 us
  transfers between devices with their start and end apart: 6, of which 6 were waited for; matrix products, arithmetic and copies ran while one was open for 4% of the time, Pallas kernels for 0%

profile of v1, /device:TPU:1, one launch (start us, length us, event | category | flops | bytes accessed | tf_op | source)
XLA Modules:
  0.0 255.0 jit_solution(17632165577815202470)
XLA Ops:
  6.5 2.0 stack.2
  8.6 5.0 %all-to-all-start = ((bf16[4,256,512]{2,1,0:T(8,128)(2,1)}), bf16[4,256,512]{2,1,0:T(8,128)(2,1)S(1)}, u32[]{:S(2)}, u32[]{:S(2)}) async-start(bf16[4,256,512]{2,1,0:T(8,128)(2,1)} %stack.2), calls=%async_computation | async-start | bytes 2097152 | tf_op jit(solution)/shard_map/all_to_all | solution.py:9
  13.8 0.1 fusion.34
  13.9 0.1 reduce_window_sum.11
  14.0 0.2 select_reduce_fusion
  14.2 12.8 %all-to-all-done = bf16[4,256,512]{2,1,0:T(8,128)(2,1)S(1)} async-done(((bf16[4,256,512]{2,1,0:T(8,128)(2,1)}), bf16[4,256,512]{2,1,0:T(8,128)(2,1)S(1)}, u32[]{:S(2)}, u32[]{:S(2)}) %all-to-all-start) | async-done | bytes 1048608 | tf_op jit(solution)/shard_map/all_to_all | solution.py:9
  27.1 0.8 copy.29
  27.9 0.8 reshape.51
  28.7 0.8 convolution_convert_fusion.1
  29.5 2.5 copy.30
  31.9 14.0 %all-to-all-start.1 = ((bf16[64,8,2048]{2,1,0:T(8,128)(2,1)}), bf16[64,8,2048]{2,1,0:T(8,128)(2,1)S(1)}, u32[]{:S(2)}, u32[]{:S(2)}) async-start(bf16[64,8,2048]{2,1,0:T(8,128)(2,1)} %copy.30), calls=%async_computation.1 | async-start | bytes 4194304 | tf_op jit(solution)/shard_map/all_to_all | solution.py:74
  46.0 0.7 all-gather.2.cloned.1.call-update
  46.7 25.8 %all-gather.2.cloned.1.call-done = bf16[256,2048]{1,0:T(8,128)(2,1)} async-done(((bf16[256,512]{1,0:T(8,128)(2,1)}), bf16[256,2048]{1,0:T(8,128)(2,1)}) %all-gather.2.cloned.1.call-update) | async-done | bytes 1048592 | tf_op jit(solution)/shard_map/all_gather | solution.py:55
  72.5 2.0 convolution_convert_fusion
  74.5 2.5 copy.31
  76.9 18.7 %all-to-all-done.1 = bf16[64,8,2048]{2,1,0:T(8,128)(2,1)S(1)} async-done(((bf16[64,8,2048]{2,1,0:T(8,128)(2,1)}), bf16[64,8,2048]{2,1,0:T(8,128)(2,1)S(1)}, u32[]{:S(2)}, u32[]{:S(2)}) %all-to-all-start.1) | async-done | bytes 2097184 | tf_op jit(solution)/shard_map/all_to_all | solution.py:74
  95.7 7.2 %all-to-all-start.2 = ((bf16[64,8,2048]{2,1,0:T(8,128)(2,1)}), bf16[64,8,2048]{2,1,0:T(8,128)(2,1)}, u32[]{:S(2)}, u32[]{:S(2)}) async-start(bf16[64,8,2048]{2,1,0:T(8,128)(2,1)} %copy.31), calls=%async_computation.2 | async-start | bytes 4194304 | tf_op jit(solution)/shard_map/all_to_all | solution.py:73
  102.8 0.2 reduce-scatter.2.cloned.1.call-start
  103.0 6.0 %fusion.8 = f32[512,1024]{1,0:T(8,128)} fusion(bf16[1,1024,2048]{2,1,0:T(8,128)(2,1)} %param.13, bf16[64,8,2048]{2,1,0:T(8,128)(2,1)S(1)} %all-to-all-done.1), kind=kOutput, calls=%fused_computation.8 | convolution fusion | flops 2147483648 | bytes 8388608 | tf_op jit(solution)/shard_map/dot_general | solution.py:16
  109.0 43.4 %all-to-all-done.2 = bf16[64,8,2048]{2,1,0:T(8,128)(2,1)} async-done(((bf16[64,8,2048]{2,1,0:T(8,128)(2,1)}), bf16[64,8,2048]{2,1,0:T(8,128)(2,1)}, u32[]{:S(2)}, u32[]{:S(2)}) %all-to-all-start.2) | async-done | bytes 2097184 | tf_op jit(solution)/shard_map/all_to_all | solution.py:73
  152.4 6.5 %fusion.2 = f32[512,1024]{1,0:T(8,128)} fusion(bf16[1,2048,1024]{2,1,0:T(8,128)(2,1)} %param.11, bf16[64,8,2048]{2,1,0:T(8,128)(2,1)} %all-to-all-done.2), kind=kOutput, calls=%fused_computation.2 | convolution fusion | flops 2147483648 | bytes 8388608 | tf_op jit(solution)/shard_map/dot_general | solution.py:14
  158.9 11.5 %fusion = f32[512,2048]{1,0:T(8,128)} fusion(bf16[1,2048,1024]{2,1,0:T(8,128)(2,1)} %param.11, f32[512,1024]{1,0:T(8,128)} %fusion.2, f32[512,1024]{1,0:T(8,128)S(1)} %copy-done.2, bf16[1,2048,1024]{2,1,0:T(8,128)(2,1)} %param.12, bf16[64,8,2048]{2,1,0:T(8,128)(2,1)} %all-to-all-done.2), kind=kOutput, calls=%fused_computation | convolution fusion | flops 4300210176 | bytes 18874368 | tf_op jit(solution)/shard_map/dot_general | solution.py:24
  170.5 6.5 %fusion.12 = bf16[64,8,2048]{2,1,0:T(8,128)(2,1)S(1)} fusion(f32[512,2048]{1,0:T(8,128)} %fusion, bf16[1,2048,1024]{2,1,0:T(8,128)(2,1)} %param.12, f32[512,1024]{1,0:T(8,128)S(1)} %copy-done.2, f32[512,1024]{1,0:T(8,128)} %fusion.2), kind=kOutput, calls=%fused_computation.13 | convolution fusion | flops 2152726528 | bytes 14680064 | tf_op jit(solution)/shard_map/dot_general | solution.py:27
  177.0 2.5 copy.32
  179.5 28.1 %reduce-scatter.2.cloned.1.call-done = bf16[64,2,2048]{2,0,1:T(8,128)(2,1)} async-done(((bf16[64,8,2048]{2,0,1:T(8,128)(2,1)}), bf16[64,2,2048]{2,0,1:T(8,128)(2,1)}) %reduce-scatter.2.cloned.1.call-update) | async-done | bytes 524304 | tf_op jit(solution)/shard_map/reduce_scatter | solution.py:84
  207.6 2.4 copy.33
  210.0 10.7 %all-to-all-start.3 = ((bf16[64,2,2048]{2,1,0:T(2,128)(2,1)}), bf16[64,2,2048]{2,1,0:T(2,128)(2,1)S(1)}, u32[]{:S(2)}, u32[]{:S(2)}) async-start(bf16[64,2,2048]{2,1,0:T(2,128)(2,1)} %copy.33), calls=%async_computation.4 | async-start | bytes 1048576 | tf_op jit(solution)/shard_map/all_to_all | solution.py:90
  220.7 17.7 %all-to-all-done.3 = bf16[64,2,2048]{2,1,0:T(2,128)(2,1)S(1)} async-done(((bf16[64,2,2048]{2,1,0:T(2,128)(2,1)}), bf16[64,2,2048]{2,1,0:T(2,128)(2,1)S(1)}, u32[]{:S(2)}, u32[]{:S(2)}) %all-to-all-start.3) | async-done | bytes 524320 | tf_op jit(solution)/shard_map/all_to_all | solution.py:90
  238.4 0.2 reshape.50
  238.6 0.3 convolution_convert_fusion.2
  238.9 8.6 %all_to_all.39 = bf16[64,4,512]{2,0,1:T(8,128)(2,1)S(1)} all-to-all(bf16[64,4,512]{2,0,1:T(8,128)(2,1)S(1)} %bitcast.67), channel_id=1, replica_groups=mesh['expert'=64,'tensor'=4] {'tensor'}, dimensions={1} | all-to-all | bytes 524288 | tf_op jit(solution)/shard_map/all_to_all | solution.py:97
  247.5 0.7 copy.41
  (14 shorter events, 0.3 us)
Async XLA Ops:
  6.5 7.0 %copy-start.1 = (s32[64]{0:T(128)S(1)}, s32[64]{0:T(128)}, u32[]{:S(2)}) copy-start(s32[64]{0:T(128)} %param.10) | copy-start | bytes 772
  6.5 7.0 %copy-start = (s32[256,1]{0,1:T(1,128)S(1)}, s32[256,1]{0,1:T(1,128)}, u32[]{:S(2)}) copy-start(s32[256,1]{0,1:T(1,128)} %param.9) | copy-start | bytes 3076
  8.6 18.5 %all-to-all-start = ((bf16[4,256,512]{2,1,0:T(8,128)(2,1)}), bf16[4,256,512]{2,1,0:T(8,128)(2,1)S(1)}, u32[]{:S(2)}, u32[]{:S(2)}) async-start(bf16[4,256,512]{2,1,0:T(8,128)(2,1)} %stack.2), calls=%async_computation | async-start | bytes 2097152 | tf_op jit(solution)/shard_map/all_to_all | solution.py:9
  31.9 63.7 %all-to-all-start.1 = ((bf16[64,8,2048]{2,1,0:T(8,128)(2,1)}), bf16[64,8,2048]{2,1,0:T(8,128)(2,1)S(1)}, u32[]{:S(2)}, u32[]{:S(2)}) async-start(bf16[64,8,2048]{2,1,0:T(8,128)(2,1)} %copy.30), calls=%async_computation.1 | async-start | bytes 4194304 | tf_op jit(solution)/shard_map/all_to_all | solution.py:74
  46.0 26.5 %all-gather.2.cloned.1.call-start = ((), (), s32[]{:S(2)}) async-start(), calls=%async_computation.6 | async-start | bytes 1310720 | tf_op jit(solution)/shard_map/all_gather | solution.py:55
  95.7 56.8 %all-to-all-start.2 = ((bf16[64,8,2048]{2,1,0:T(8,128)(2,1)}), bf16[64,8,2048]{2,1,0:T(8,128)(2,1)}, u32[]{:S(2)}, u32[]{:S(2)}) async-start(bf16[64,8,2048]{2,1,0:T(8,128)(2,1)} %copy.31), calls=%async_computation.2 | async-start | bytes 4194304 | tf_op jit(solution)/shard_map/all_to_all | solution.py:73
  102.8 104.8 %reduce-scatter.2.cloned.1.call-start = ((), (), s32[]{:S(2)}) async-start(), calls=%async_computation.7 | async-start | bytes 2621440 | tf_op jit(solution)/shard_map/reduce_scatter | solution.py:84
  109.0 49.9 %copy-start.2 = (f32[512,1024]{1,0:T(8,128)S(1)}, f32[512,1024]{1,0:T(8,128)}, u32[]{:S(2)}) copy-start(f32[512,1024]{1,0:T(8,128)} %fusion.8) | copy-start | bytes 6291460
  210.0 28.4 %all-to-all-start.3 = ((bf16[64,2,2048]{2,1,0:T(2,128)(2,1)}), bf16[64,2,2048]{2,1,0:T(2,128)(2,1)S(1)}, u32[]{:S(2)}, u32[]{:S(2)}) async-start(bf16[64,2,2048]{2,1,0:T(2,128)(2,1)} %copy.33), calls=%async_computation.4 | async-start | bytes 1048576 | tf_op jit(solution)/shard_map/all_to_all | solution.py:90
Sparse Core Ops, SparseCore 0:
  48.6 23.8 all-gather.1
  179.6 27.9 reduce-scatter.1
